TPU v7x, 32 devices: a whole 2x2x4 slice. The times are simulated.
32 devices in a mesh: slab: 8 (over z, x), row: 4 (over y, core).
Axes of the slice: x: 2, y: 2, z: 4, core: 2. Of those that a mesh axis runs over, the one named last changes fastest.
Arguments:
- image: bfloat16 [32, 128, 8], P('slab', 'row'), may hold values from -6 to 6
- first_kernel: bfloat16 [3, 3, 32, 1], replicated, may hold values from -2 to 2
- first_bias: float32 [32], replicated, may hold values from -1.5 to 1.5
- middle_kernel: bfloat16 [3, 3, 32, 32], replicated, may hold values from -0.5 to 0.5
- middle_bias: float32 [32], replicated, may hold values from -1.5 to 1.5
- last_kernel: bfloat16 [3, 3, 3, 32], replicated, may hold values from -0.5 to 0.5
- last_bias: float32 [3], replicated, may hold values from -2 to 2
Outputs:
- flows: float32 [4, 32, 128, 8], P(None, 'slab', 'row')
All inputs are finite; a program needn't handle non-finite values.
Results may differ from a plain program's by a relative error of at most 0.0052.
Values may be sent and summed in bfloat16 or wider, within the bound.
No kernel may reach another device: no remote copies, remote signals or barrier semaphores. Data moves between devices by JAX's collectives and lax.ppermute only.
A program may use at most 64 MiB of HBM per device.

v0:
```python
import jax
import jax.numpy as jnp
from jax import lax
from jax.sharding import PartitionSpec as P


def with_halo(array, sides, width):
    for axis, dim in sides:
        devices, length = (lax.axis_size(axis), array.shape[dim])
        up = [(i, (i + 1) % devices) for i in range(devices - 1)]
        down = [(j, i) for i, j in up]
        last = lax.slice_in_dim(array, length - width, length, axis=dim)
        initial = lax.slice_in_dim(array, 0, width, axis=dim)
        before = lax.ppermute(last, axis, up)
        after = lax.ppermute(initial, axis, down)
        array = jnp.concatenate([before, array, after], axis=dim)
    return array


def flatten_kernel(kernel):
    outputs = kernel.shape[2]
    inputs = kernel.shape[3]
    return kernel.transpose(2, 0, 1, 3).reshape(outputs, 9 * inputs)


def apply_layer(values, kernel, bias):
    rows = values.shape[1] - 2
    cols = values.shape[2] - 2
    taps = []
    for row_shift in range(3):
        for col_shift in range(3):
            sliced = lax.slice_in_dim(values, row_shift, row_shift + rows, axis=1)
            taps.append(lax.slice_in_dim(sliced, col_shift, col_shift + cols, axis=2))
    stacked = jnp.concatenate(taps, axis=0)
    result = jnp.einsum("ok,k...->o...", kernel, stacked, preferred_element_type=jnp.float32)
    return result + bias.reshape((-1,) + (1,) * (values.ndim - 1))


def keep_inside(values, axis_pos, anchor, limit):
    coords = anchor + jnp.arange(values.shape[axis_pos], dtype=jnp.int32)
    inside = ((coords >= 0) & (coords < limit)).astype(values.dtype)
    shape = [1] * values.ndim
    shape[axis_pos] = values.shape[axis_pos]
    return values * inside.reshape(shape)


def forward(plane, kernels, biases):
    rows_local = plane.shape[1]
    y_total = rows_local * lax.axis_size("row")
    y_anchor = lax.axis_index("row") * rows_local
    current = with_halo(plane, (("row", 1),), 3)
    y_anchor = y_anchor - 3
    for level_index in range(3):
        padding = [(0, 0), (0, 0), (1, 1)] + [(0, 0)] * (current.ndim - 3)
        current = jnp.pad(current, padding)
        result = apply_layer(current, kernels[level_index], biases[level_index])
        if level_index == 2:
            return result
        result = jax.nn.relu(result)
        y_anchor = y_anchor + 1
        result = keep_inside(result, 1, y_anchor, y_total)
        current = result.astype(jnp.bfloat16)
    return current


def local(image, first_kernel, first_bias, middle_kernel, middle_bias, last_kernel, last_bias):
    weights = (first_kernel, middle_kernel, last_kernel)
    biases = (first_bias, middle_bias, last_bias)
    kernels_xy = [flatten_kernel(weight) for weight in weights]
    kernels_yz = [flatten_kernel(weight.transpose(1, 0, 2, 3)) for weight in weights]
    xy_planes = image.transpose(1, 2, 0)[None]
    xy_flows = forward(xy_planes, kernels_xy, biases)
    xy_moved = xy_flows.transpose(0, 3, 1, 2)
    columns = lax.all_to_all(image, "slab", split_axis=2, concat_axis=0, tiled=True)
    yz_planes = columns.transpose(1, 0, 2)[None]
    yz_columns = forward(yz_planes, kernels_yz, biases)
    returned = lax.all_to_all(yz_columns, "slab", split_axis=2, concat_axis=3, tiled=True)
    yz_flows = returned.transpose(0, 2, 1, 3)
    return jnp.stack(
        [
            yz_flows[0],
            0.5 * (xy_moved[0] + yz_flows[1]),
            xy_moved[1],
            0.5 * (xy_moved[2] + yz_flows[2]),
        ]
    )


def solution(mesh):
    placed = (P("slab", "row", None), P(), P(), P(), P(), P(), P())
    return jax.shard_map(
        local, mesh=mesh, in_specs=placed, out_specs=P(None, "slab", "row", None), check_vma=False
    )
```

profile of v0, /device:TPU:1, one launch (start us, length us, event | category | flops | bytes accessed | tf_op | source)
XLA Modules:
  0.0 52.4 jit_solution(10197623291869757960)
XLA Ops:
  0.0 0.7 %copy.148 = bf16[1,32,8,4]{1,0,3,2:T(2,128)(2,1)S(1)} copy(bf16[1,32,8,4]{1,2,3,0:T(8,128)(2,1)} %bitcast.97) | data formatting | bytes 4096 | tf_op jit(solution)/shard_map/broadcast_in_dim | solution.py:71
  0.8 4.5 %collective-permute-start.2 = (bf16[1,3,8,4]{1,0,3,2:T(2,128)(2,1)S(1)}, bf16[1,3,8,4]{1,0,3,2:T(2,128)(2,1)S(1)}, u32[]{:S(2)}, u32[]{:S(2)}) collective-permute-start(bf16[1,3,8,4]{1,0,3,2:T(2,128)(2,1)S(1)} %get-tuple-element.18), channel_id=1, source_target_pairs={{0,1},{1,2},{2,3},{4,5},{5,6},{6,7},{8,9},{9,10},{10,11},{12,13},{... | collective-permute-start | bytes 584 | tf_op jit(solution)/shard_map/ppermute | solution.py:14
  5.3 1.9 %collective-permute-start.3 = (bf16[1,3,8,4]{1,0,3,2:T(2,128)(2,1)S(1)}, bf16[1,3,8,4]{1,0,3,2:T(2,128)(2,1)S(1)}, u32[]{:S(2)}, u32[]{:S(2)}) collective-permute-start(bf16[1,3,8,4]{1,0,3,2:T(2,128)(2,1)S(1)} %get-tuple-element.19), channel_id=1, source_target_pairs={{1,0},{2,1},{3,2},{5,4},{6,5},{7,6},{9,8},{10,9},{11,10},{13,12},{... | collective-permute-start | bytes 584 | tf_op jit(solution)/shard_map/ppermute | solution.py:15
  7.3 1.3 %copy.135 = bf16[4,32,8]{1,0,2:T(4,128)(2,1)} copy(bf16[4,32,8]{1,2,0:T(8,128)(2,1)} %param.7) | data formatting | bytes 4096 | tf_op args[0]
  8.6 5.5 %all-to-all-start = ((bf16[4,32,8]{1,0,2:T(4,128)(2,1)}), bf16[4,32,8]{1,0,2:T(4,128)(2,1)S(1)}, u32[]{:S(2)}, u32[]{:S(2)}) async-start(bf16[4,32,8]{1,0,2:T(4,128)(2,1)} %copy.135), calls=%async_computation | async-start | bytes 16384 | tf_op jit(solution)/shard_map/all_to_all | solution.py:74
  14.1 0.7 %reshape.81 = bf16[32,9,1,1]{0,1,2,3:T(8,128)(2,1)S(1)} reshape(bf16[32,3,3,1]{0,2,3,1:T(4,128)(2,1)} %bitcast.100) | data formatting | bytes 1152 | tf_op jit(solution)/shard_map/reshape | solution.py:23
  14.8 0.9 %copy.151 = bf16[32,3,3,32]{3,2,1,0:T(4,128)(2,1)S(1)} copy(bf16[32,3,3,32]{3,0,2,1:T(8,128)(2,1)} %bitcast.89) | data formatting | bytes 36864 | tf_op jit(solution)/shard_map/transpose | solution.py:23
  15.9 0.7 %copy.153 = bf16[3,3,3,32]{3,2,1,0:T(4,128)(2,1)S(1)} copy(bf16[3,3,3,32]{3,0,2,1:T(4,128)(2,1)} %bitcast.95) | data formatting | bytes 3456 | tf_op jit(solution)/shard_map/transpose | solution.py:23
  16.7 0.7 %copy.140 = bf16[32,3,3,1]{0,2,1,3:T(4,128)(2,1)S(1)} copy(bf16[32,3,3,1]{0,1,3,2:T(4,128)(2,1)} %bitcast.101) | data formatting | bytes 1152 | tf_op jit(solution)/shard_map/transpose;transpose | solution.py:23
  17.4 0.9 %copy.141 = bf16[32,3,3,32]{3,2,1,0:T(4,128)(2,1)S(1)} copy(bf16[32,3,3,32]{3,0,1,2:T(8,128)(2,1)} %bitcast.90) | data formatting | bytes 36864 | tf_op jit(solution)/shard_map/transpose;transpose | solution.py:23
  18.4 0.7 %copy.143 = bf16[3,3,3,32]{3,2,1,0:T(4,128)(2,1)S(1)} copy(bf16[3,3,3,32]{3,0,1,2:T(4,128)(2,1)} %bitcast.96) | data formatting | bytes 3456 | tf_op jit(solution)/shard_map/transpose;transpose | solution.py:23
  19.3 0.2 pad_slice_fusion.12
  19.5 0.2 concatenate.29
  19.8 0.9 %fusion.26 = bf16[32,36,8,4]{1,0,3,2:T(8,128)(2,1)S(1)} fusion(bf16[9,36,8,4]{1,0,3,2:T(8,128)(2,1)S(1)} %concatenate.29, f32[36]{0:T(128)S(1)} %and_convert_fusion.1, f32[32]{0:T(128)} %param.9, bf16[32,9,1,1]{0,1,2,3:T(8,128)(2,1)S(1)} %reshape.81), kind=kOutput, calls=%fused_computation.21 | convolution fusion | flops 811008 | bytes 95312 | tf_op jit(solution)/shard_map/ok,k...->o.../dot_general | solution.py:35
  20.9 0.2 fusion.39
  21.1 0.2 slice_dynamic-update-slice_fusion.4
  21.3 0.2 fusion.40
  21.5 0.2 fusion.41
  21.7 0.2 slice_dynamic-update-slice_fusion.3
  22.1 0.5 %fusion.30 = bf16[32,34,8,4]{1,0,3,2:T(8,128)(2,1)S(1)} fusion(bf16[288,34,8,4]{1,0,3,2:T(8,128)(2,1)S(1)} %fusion.42, f32[34]{0:T(128)S(1)} %and_convert_fusion, f32[32]{0:T(128)S(1)} %copy-done, bf16[32,288,1,1]{1,0,2,3:T(8,128)(2,1)S(1)} %reshape.82), kind=kOutput, calls=%fused_computation.23 | convolution fusion | flops 20193280 | bytes 715016 | tf_op jit(solution)/shard_map/ok,k...->o.../dot_general | solution.py:35
  22.8 0.2 fusion.45
  23.0 0.2 slice_dynamic-update-slice_fusion.1
  23.2 0.2 fusion.46
  23.6 0.2 slice_dynamic-update-slice_fusion
  23.8 0.2 fusion.48
  24.3 3.9 %collective-permute-start = (bf16[1,3,32,1]{1,0,2,3:T(2,128)(2,1)S(1)}, bf16[1,3,32,1]{1,0,2,3:T(2,128)(2,1)S(1)}, u32[]{:S(2)}, u32[]{:S(2)}) collective-permute-start(bf16[1,3,32,1]{1,0,2,3:T(2,128)(2,1)S(1)} %get-tuple-element.29), channel_id=1, source_target_pairs={{0,1},{1,2},{2,3},{4,5},{5,6},{6,7},{8,9},{9,10},{10,11},{12,13},{... | collective-permute-start | bytes 584 | tf_op jit(solution)/shard_map/ppermute | solution.py:14
  28.2 1.9 %collective-permute-start.1 = (bf16[1,3,32,1]{1,0,2,3:T(2,128)(2,1)S(1)}, bf16[1,3,32,1]{1,0,2,3:T(2,128)(2,1)S(1)}, u32[]{:S(2)}, u32[]{:S(2)}) collective-permute-start(bf16[1,3,32,1]{1,0,2,3:T(2,128)(2,1)S(1)} %get-tuple-element.30), channel_id=1, source_target_pairs={{1,0},{2,1},{3,2},{5,4},{6,5},{7,6},{9,8},{10,9},{11,10},{13,12},{... | collective-permute-start | bytes 584 | tf_op jit(solution)/shard_map/ppermute | solution.py:15
  30.2 0.4 fusion.55
  30.6 2.7 %collective-permute-done.1 = bf16[1,3,32,1]{1,0,2,3:T(2,128)(2,1)S(1)} collective-permute-done((bf16[1,3,32,1]{1,0,2,3:T(2,128)(2,1)S(1)}, bf16[1,3,32,1]{1,0,2,3:T(2,128)(2,1)S(1)}, u32[]{:S(2)}, u32[]{:S(2)}) %collective-permute-start.1) | collective-permute-done | bytes 224 | tf_op jit(solution)/shard_map/ppermute | solution.py:15
  33.4 0.2 pad_slice_fusion.18
  33.6 0.2 concatenate.25
  33.9 0.3 fusion.25
  34.5 0.2 slice_dynamic-update-slice_fusion.10
  34.9 0.2 slice_dynamic-update-slice_fusion.19
  35.1 0.2 slice_dynamic-update-slice_fusion.9
  35.2 0.2 slice_dynamic-update-slice_fusion.18
  35.4 0.5 %fusion.27 = bf16[32,34,32,1]{1,0,2,3:T(8,128)(2,1)S(1)} fusion(bf16[32,288,1]{1,0,2:T(8,128)(2,1)S(1)} %reshape.79, bf16[288,34,32,1]{1,0,2,3:T(8,128)(2,1)S(1)} %slice_dynamic-update-slice_fusion.18, f32[34]{0:T(128)S(1)} %and_convert_fusion, f32[32]{0:T(128)S(1)} %copy-done), kind=kOutput, calls=%fused_computation.22 | convolution fusion | flops 20193280 | bytes 715016 | tf_op jit(solution)/shard_map/ok,k...->o.../dot_general | solution.py:35
  36.4 0.2 slice_dynamic-update-slice_fusion.7
  36.7 0.2 slice_dynamic-update-slice_fusion.13
  37.1 0.2 slice_dynamic-update-slice_fusion.12
  37.3 0.4 fusion.34
  37.8 0.5 %broadcast.97 = f32[]{:T(128)} broadcast(f32[]{:T(128)} %constant.164), dimensions={} | broadcast | bytes 8
  38.3 0.8 %reduce = f32[32,3,32]{2,1,0:T(4,128)S(1)} reduce(f32[32,3,1,32]{3,2,1,0:T(1,128)S(1)} %bitcast.91, f32[]{:T(128)} %broadcast.97), dimensions={2}, to_apply=%bitcast.88.reduce_sub_computation | reduce | bytes 24580
  39.1 0.7 %reshape.90 = f32[8,1,384]{2,1,0:T(1,128)} reshape(f32[32,3,32]{2,1,0:T(4,128)S(1)} %reduce) | data formatting | bytes 24576
  39.8 5.7 %all-to-all-start.1 = ((f32[8,1,384]{2,1,0:T(1,128)}), f32[8,1,384]{2,1,0:T(1,128)S(1)}, u32[]{:S(2)}, u32[]{:S(2)}) async-start(f32[8,1,384]{2,1,0:T(1,128)} %reshape.90), calls=%async_computation.1 | async-start | bytes 24576 | tf_op jit(solution)/shard_map/all_to_all | solution.py:77
  45.6 5.3 %all-to-all-done.1 = f32[8,1,384]{2,1,0:T(1,128)S(1)} async-done(((f32[8,1,384]{2,1,0:T(1,128)}), f32[8,1,384]{2,1,0:T(1,128)S(1)}, u32[]{:S(2)}, u32[]{:S(2)}) %all-to-all-start.1) | async-done | bytes 12320 | tf_op jit(solution)/shard_map/all_to_all | solution.py:77
  50.9 0.7 %reduce.1 = f32[8,384]{1,0:T(8,128)S(1)} reduce(f32[8,1,384]{2,1,0:T(1,128)S(1)} %all-to-all-done.1, f32[]{:T(128)} %broadcast.97), dimensions={1}, to_apply=%all_to_all.30.reduce_sub_computation | reduce | bytes 24580 | tf_op jit(solution)/shard_map/all_to_all | solution.py:77
  51.7 0.6 %pad_maximum_fusion = f32[4,4,32,8]{2,3,1,0:T(8,128)} fusion(f32[1,4,32,8]{2,3,1,0:T(8,128)S(1)} %get-tuple-element.6, f32[1,4,32,8]{2,3,1,0:T(8,128)S(1)} %get-tuple-element.8, f32[1,4,32,8]{2,3,1,0:T(8,128)S(1)} %get-tuple-element.5, f32[1,4,32,8]{2,3,1,0:T(8,128)S(1)} %get-tuple-element.7), kind=kLoop, calls=%fused_computation.75 | loop fusion | flops 12288 | bytes 32768 | tf_op jit(solution)/shard_map/stack | solution.py:79
  (48 shorter events, 3.2 us)
Async XLA Ops:
  0.8 18.4 %collective-permute-start.2 = (bf16[1,3,8,4]{1,0,3,2:T(2,128)(2,1)S(1)}, bf16[1,3,8,4]{1,0,3,2:T(2,128)(2,1)S(1)}, u32[]{:S(2)}, u32[]{:S(2)}) collective-permute-start(bf16[1,3,8,4]{1,0,3,2:T(2,128)(2,1)S(1)} %get-tuple-element.18), channel_id=1, source_target_pairs={{0,1},{1,2},{2,3},{4,5},{5,6},{6,7},{8,9},{9,10},{10,11},{12,13},{... | collective-permute-start | bytes 584 | tf_op jit(solution)/shard_map/ppermute | solution.py:14
  5.3 13.9 %collective-permute-start.3 = (bf16[1,3,8,4]{1,0,3,2:T(2,128)(2,1)S(1)}, bf16[1,3,8,4]{1,0,3,2:T(2,128)(2,1)S(1)}, u32[]{:S(2)}, u32[]{:S(2)}) collective-permute-start(bf16[1,3,8,4]{1,0,3,2:T(2,128)(2,1)S(1)} %get-tuple-element.19), channel_id=1, source_target_pairs={{1,0},{2,1},{3,2},{5,4},{6,5},{7,6},{9,8},{10,9},{11,10},{13,12},{... | collective-permute-start | bytes 584 | tf_op jit(solution)/shard_map/ppermute | solution.py:15
  8.6 15.4 %all-to-all-start = ((bf16[4,32,8]{1,0,2:T(4,128)(2,1)}), bf16[4,32,8]{1,0,2:T(4,128)(2,1)S(1)}, u32[]{:S(2)}, u32[]{:S(2)}) async-start(bf16[4,32,8]{1,0,2:T(4,128)(2,1)} %copy.135), calls=%async_computation | async-start | bytes 16384 | tf_op jit(solution)/shard_map/all_to_all | solution.py:74
  20.7 1.4 %copy-start = (f32[32]{0:T(128)S(1)}, f32[32]{0:T(128)}, u32[]{:S(2)}) copy-start(f32[32]{0:T(128)} %param.11) | copy-start | bytes 388
  23.4 10.5 %copy-start.2 = (f32[32]{0:T(128)S(1)}, f32[32]{0:T(128)}, u32[]{:S(2)}) copy-start(f32[32]{0:T(128)} %param.9) | copy-start | bytes 388
  24.3 6.3 %collective-permute-start = (bf16[1,3,32,1]{1,0,2,3:T(2,128)(2,1)S(1)}, bf16[1,3,32,1]{1,0,2,3:T(2,128)(2,1)S(1)}, u32[]{:S(2)}, u32[]{:S(2)}) collective-permute-start(bf16[1,3,32,1]{1,0,2,3:T(2,128)(2,1)S(1)} %get-tuple-element.29), channel_id=1, source_target_pairs={{0,1},{1,2},{2,3},{4,5},{5,6},{6,7},{8,9},{9,10},{10,11},{12,13},{... | collective-permute-start | bytes 584 | tf_op jit(solution)/shard_map/ppermute | solution.py:14
  28.2 5.1 %collective-permute-start.1 = (bf16[1,3,32,1]{1,0,2,3:T(2,128)(2,1)S(1)}, bf16[1,3,32,1]{1,0,2,3:T(2,128)(2,1)S(1)}, u32[]{:S(2)}, u32[]{:S(2)}) collective-permute-start(bf16[1,3,32,1]{1,0,2,3:T(2,128)(2,1)S(1)} %get-tuple-element.30), channel_id=1, source_target_pairs={{1,0},{2,1},{3,2},{5,4},{6,5},{7,6},{9,8},{10,9},{11,10},{13,12},{... | collective-permute-start | bytes 584 | tf_op jit(solution)/shard_map/ppermute | solution.py:15
  36.0 1.3 %copy-start.1 = (f32[3]{0:T(128)S(1)}, f32[3]{0:T(128)}, u32[]{:S(2)}) copy-start(f32[3]{0:T(128)} %param.13) | copy-start | bytes 40
  39.8 11.1 %all-to-all-start.1 = ((f32[8,1,384]{2,1,0:T(1,128)}), f32[8,1,384]{2,1,0:T(1,128)S(1)}, u32[]{:S(2)}, u32[]{:S(2)}) async-start(f32[8,1,384]{2,1,0:T(1,128)} %reshape.90), calls=%async_computation.1 | async-start | bytes 24576 | tf_op jit(solution)/shard_map/all_to_all | solution.py:77
where the time goes:
time: 53 us; the launch traced here: 52.4 us
  starting transfers between devices  23.5 us (44%)
  local copies, waits for them, and re-layouts  14.8 us (28%)
  waiting for transfers between devices  8.04 us (15%)
  matrix products  3.14 us (6%)
  other arithmetic  2.4 us (5%)
    ppermute x2, starting transfers between devices, with_halo(): before = lax.ppermute(last, axis, up)  8.45 us
    unnamed x42, local copies, waits for them, and re-layouts  6.96 us
    all_to_all x1, starting transfers between devices, local(): lax.all_to_all(yz_columns, 'slab', split_axis=2, concat_axis=3, tiled=True)  5.7 us
    all_to_all x1, starting transfers between devices, local(): lax.all_to_all(image, 'slab', split_axis=2, concat_axis=0, tiled=True)  5.53 us
    all_to_all x1, waiting for transfers between devices, local(): lax.all_to_all(yz_columns, 'slab', split_axis=2, concat_axis=3, tiled=True)  5.33 us
    ppermute x2, starting transfers between devices, with_halo(): after = lax.ppermute(initial, axis, down)  3.84 us
    dot_general x6, matrix products, apply_layer(): jnp.einsum('ok,k...->o...', kernel, stacked, preferred_element_type=jnp.f...  3.14 us
    ppermute x2, waiting for transfers between devices, with_halo(): after = lax.ppermute(initial, axis, down)  2.71 us
  transfers between devices with their start and end apart: 6, of which 2 were waited for; matrix products, arithmetic and copies ran while one was open for 22% of the time, Pallas kernels for 0%

commit v1 on v0

v1 whole, which is shorter than its diff:
```python
import functools

import jax
import jax.numpy as jnp
from jax import lax
from jax.experimental import pallas as pl
from jax.experimental.pallas import tpu as pltpu
from jax.sharding import PartitionSpec as P

SUB = 8
LANES = 128
NEVER = -3.0e38
LIMIT = 12 << 20
F32 = jnp.float32
BF16 = jnp.bfloat16


def matching(count, parity):
    partner = {}
    for left in range(parity, count - 1, 2):
        partner[left] = left + 1
        partner[left + 1] = left
    return partner


def swap_rows(values, parity):
    count = lax.axis_size("row")
    partner = matching(count, parity)
    ends = [i for i in range(count) if i not in partner]
    for here, there in zip(ends, reversed(ends)):
        partner[here] = there
    return lax.ppermute(values, "row", sorted(partner.items()))


def swap_slabs(values, parity):
    slabs, rows = lax.axis_size("slab"), lax.axis_size("row")
    partner = matching(slabs, parity)
    across = matching(rows, 0)
    pairs = []
    for s in range(slabs):
        for r in range(rows):
            there = (partner[s], r) if s in partner else (s, across.get(r, r))
            pairs.append((s * rows + r, there[0] * rows + there[1]))
    return lax.ppermute(values, ("slab", "row"), pairs)


def before_and_after(even, odd, axis):
    here, count = lax.axis_index(axis), lax.axis_size(axis)
    low = here % 2 == 0
    before = jnp.where(low, odd, even)
    after = jnp.where(low, even, odd)
    before = jnp.where(here > 0, before, jnp.zeros_like(before))
    after = jnp.where(here < count - 1, after, jnp.zeros_like(after))
    return before, after


def tile_lanes(row, count):
    return jnp.concatenate([row] * count, axis=1)


def iota(shape, dim):
    return lax.broadcasted_iota(jnp.int32, shape, dim)


def nn(left, right):
    return lax.dot_general(left, right, (((1,), (0,)), ((), ())), preferred_element_type=F32)


def nt(left, right):
    return lax.dot_general(left, right, (((1,), (1,)), ((), ())), preferred_element_type=F32)


def keep_hidden(scratch, values):
    for i in range(0, values.shape[1], LANES):
        piece = values[:, i : i + LANES]
        scratch[i // LANES][:, : piece.shape[1]] = piece


def gather_hidden(scratch, starts, count, lanes):
    columns = []
    for i in range(0, lanes, LANES):
        parts = [scratch[i // LANES][pl.ds(start, count, stride=SUB), :] for start in starts]
        columns.append(jnp.concatenate(parts, axis=0).astype(BF16)[:, : lanes - i])
    return jnp.concatenate(columns, axis=1)


class Sizes:
    def __init__(self, slices, rows, cols, channels, outputs, slabs, parts):
        self.slices, self.rows, self.cols = slices, rows, cols
        self.channels, self.outputs = channels, outputs
        self.slabs, self.parts = slabs, parts
        assert slices >= 3 and SUB % slices == 0
        self.halves = SUB // slices
        assert rows % self.halves == 0 and cols % SUB == 0
        self.span = rows // self.halves
        self.chunks = []
        self.kinds = []
        for start in range(0, cols, SUB):
            ranges = []
            for reach in (3, 2, 1, 0):
                low = max(0, start - reach)
                ranges.append((low - start, min(cols, start + SUB + reach) - low))
            kind = tuple(ranges)
            if kind not in self.kinds:
                self.kinds.append(kind)
            self.chunks.append((start, self.kinds.index(kind)))

    def weight_shapes(self):
        c, z = self.channels, self.slices
        shapes = [
            ((3, 3 * z * SUB, (z + 4) * c), BF16),
            ((3, (z + 2) * c, (z + 4) * c), BF16),
            ((3, self.outputs * z, (z + 2) * c), BF16),
            ((1, (z + 4) * c), F32),
            ((1, (z + 2) * c), F32),
        ]
        for image, one, two, _ in self.kinds:
            shapes += [
                ((3, z * image[1], one[1] * c), BF16),
                ((3, two[1] * c, one[1] * c), BF16),
                ((3, self.outputs * SUB, two[1] * c), BF16),
                ((1, one[1] * c), F32),
                ((1, two[1] * c), F32),
            ]
        return shapes + [((self.outputs, SUB, self.rows), F32)]


def banded(blocks, out_count, in_count, offset):
    zero = jnp.zeros_like(blocks[0])
    lines = []
    for out in range(out_count):
        line = []
        for inner in range(in_count):
            tap = inner - out + offset
            line.append(blocks[tap] if 0 <= tap < 3 else zero)
        lines.append(jnp.concatenate(line, axis=1))
    return jnp.concatenate(lines, axis=0)


def spread(rows_of, tap_of, shape, lines):
    total = jnp.zeros(shape, F32)
    for (group, tap), line in lines.items():
        here = tap_of == tap
        if rows_of is not None:
            here = here & (rows_of == group)
        total = jnp.where(here, line, total)
    return total.astype(BF16)


def prepare_kernel(sizes, t_ref, k1_ref, b1_ref, k2_ref, b2_ref, k3_ref, b3_ref, t_out, *outs):
    c, z, n_out = sizes.channels, sizes.slices, sizes.outputs
    t_out[...] = t_ref[...]
    k1 = k1_ref[...].astype(F32)
    k3 = k3_ref[...].astype(F32)
    b1, b2 = b1_ref[...], b2_ref[...]

    def first(shape, tap_of, tap_index):
        count = shape[1] // c
        lines = {(0, t): tile_lanes(k1[tap_index(t)[0], tap_index(t)[1]][None, :], count) for t in range(3)}
        return spread(None, tap_of, shape, lines)

    def last(shape, group_of, tap_of, tap_index):
        count = shape[1] // c
        lines = {}
        for g in range(n_out):
            for t in range(3):
                a, b = tap_index(t)
                lines[g, t] = tile_lanes(k3[a, b, g][None, :], count)
        return spread(group_of, tap_of, shape, lines)

    w1, w2, w3, c1, c2 = outs[:5]
    for b in range(3):
        shape = w1.shape[1:]
        tap = iota(shape, 0) // SUB - iota(shape, 1) // c + (3 - z)
        w1[b] = first(shape, tap, lambda t, b=b: (t, b))
        w2[b] = banded([k2_ref[a, b] for a in range(3)], z + 2, z + 4, 0)
        shape = w3.shape[1:]
        row = iota(shape, 0)
        w3[b] = last(shape, row // z, iota(shape, 1) // c - row % z, lambda t, b=b: (t, b))
    base = lax.axis_index("slab") * z
    for ref, bias, reach in ((c1, b1, 2), (c2, b2, 1)):
        where = base + iota(ref.shape, 1) // c - reach
        inside = (where >= 0) & (where < sizes.slabs * z)
        ref[...] = jnp.where(inside, tile_lanes(bias, ref.shape[1] // c), NEVER)

    for index, (image, one, two, out) in enumerate(sizes.kinds):
        w1, w2, w3, c1, c2 = outs[5 + 5 * index : 10 + 5 * index]
        for a in range(3):
            shape = w1.shape[1:]
            tap = iota(shape, 0) % image[1] + image[0] - iota(shape, 1) // c - one[0] + 1
            w1[a] = first(shape, tap, lambda t, a=a: (a, t))
            w2[a] = banded([k2_ref[a, b] for b in range(3)], two[1], one[1], one[0] - two[0] + 1)
            shape = w3.shape[1:]
            row = iota(shape, 0)
            tap = iota(shape, 1) // c + two[0] - row % SUB - out[0] + 1
            w3[a] = last(shape, row // SUB, tap, lambda t, a=a: (a, t))
        c1[...] = tile_lanes(b1, one[1])
        c2[...] = tile_lanes(b2, two[1])
    for g in range(n_out):
        outs[-1][g] = jnp.broadcast_to(b3_ref[0:1, g : g + 1], (SUB, sizes.rows))


def extend_kernel(own_ref, even_ref, odd_ref, out_ref):
    rows = own_ref.shape[2]
    before, after = before_and_after(even_ref[...], odd_ref[...], "row")
    out_ref[...] = jnp.concatenate([before[:, :, rows - 3 :], own_ref[...], after[:, :, :3]], axis=2)


def zero_groups(values, count, low, high):
    edge = count * SUB
    top, middle, bottom = values[:edge], values[edge:-edge], values[-edge:]
    if low.ndim:
        low, high = low[:edge], high[:edge]
    return jnp.concatenate([jnp.where(low, 0.0, top), middle, jnp.where(high, 0.0, bottom)], axis=0)


def taps(values, count):
    low, high = values.astype(BF16), values[SUB:].astype(BF16)
    return [low[:count], high[:count], low[2 * SUB : 2 * SUB + count]]


def hidden_layers(picked, groups, w1, w2, c1, c2, low, high):
    n1, n2 = (groups - 2) * SUB, (groups - 4) * SUB
    one = sum(nn(tap, w1[i]) for i, tap in enumerate(taps(picked, n1)))
    one = zero_groups(jnp.maximum(one + c1[...], 0.0), 2, low, high)
    two = sum(nt(tap, w2[i]) for i, tap in enumerate(taps(one, n2)))
    return zero_groups(jnp.maximum(two + c2[...], 0.0), 1, low, high)


def xy_kernel(sizes, e_ref, *refs):
    count = sum(1 for _ in sizes.kinds) * 5
    weights, (b3, out_ref, *hidden) = refs[:count], refs[count:]
    z, span = sizes.slices, sizes.span
    wide = sizes.rows + 6
    groups = span + 6
    row = lax.axis_index("row")
    half = iota((2 * SUB, 1), 0) % SUB // z
    low = (row == 0) & (half == 0)
    high = (row == sizes.parts - 1) & (half == sizes.halves - 1)
    shape = (groups * SUB, wide)
    wanted = iota(shape, 0) // SUB + iota(shape, 0) % SUB // z * span
    select = jnp.where(iota(shape, 1) == wanted, 1.0, 0.0).astype(BF16)
    for start, index in sizes.chunks:
        image = sizes.kinds[index][0]
        w1, w2, w3, c1, c2 = weights[5 * index : 5 * index + 5]
        low_col = start + image[0]
        e = e_ref[:, low_col : low_col + image[1], :].reshape(z * image[1], wide)
        picked = nt(select, e)
        same = iota(picked.shape, 1) // image[1] == iota(picked.shape, 0) % z
        picked = jnp.where(same, picked, 0.0)
        second = hidden_layers(picked, groups, w1, w2, c1, c2, low, high)
        keep_hidden(hidden, second)
        total = None
        for a in range(3):
            starts = [SUB * a + h * z + s for s in range(z) for h in range(sizes.halves)]
            term = nt(w3[a], gather_hidden(hidden, starts, span, second.shape[1]))
            total = term if total is None else total + term
        for g in range(sizes.outputs):
            for s in range(z):
                piece = total[g * SUB : (g + 1) * SUB, s * sizes.rows : (s + 1) * sizes.rows]
                out_ref[g, s, start : start + SUB, :] = piece + b3[g]


def yz_kernel(sizes, e_ref, even_ref, odd_ref, xy_ref, w1, w2, w3, c1, c2, b3, out_ref, turned, *hidden):
    z = sizes.slices
    wide = sizes.rows + 6
    groups = sizes.rows + 6
    row = lax.axis_index("row")
    low, high = row == 0, row == sizes.parts - 1
    before, after = before_and_after(even_ref[...], odd_ref[...], "slab")
    block = jnp.concatenate([before, e_ref[...], after], axis=0)
    shape = (groups * SUB, wide)
    select = jnp.where(iota(shape, 1) == iota(shape, 0) // SUB, 1.0, 0.0).astype(BF16)
    for start in range(0, sizes.cols, SUB):
        e = block[:, start : start + SUB, :].reshape(3 * z * SUB, wide)
        picked = nt(select, e)
        same = iota(picked.shape, 1) % SUB == iota(picked.shape, 0) % SUB
        picked = jnp.where(same, picked, 0.0)
        two = hidden_layers(picked, groups, w1, w2, c1, c2, low, high)
        keep_hidden(hidden, two)
        total = None
        for b in range(3):
            starts = [SUB * b + x for x in range(SUB)]
            term = nt(w3[b], gather_hidden(hidden, starts, sizes.rows, two.shape[1]))
            total = term if total is None else total + term
        rest = jnp.zeros((total.shape[0], LANES - sizes.rows), F32)
        for x in range(SUB):
            piece = total[:, x * sizes.rows : (x + 1) * sizes.rows]
            turned[pl.ds(x, total.shape[0], stride=SUB), :] = jnp.concatenate([piece, rest], axis=1)
        for s in range(z):
            yz = [turned[(g * z + s) * SUB : (g * z + s + 1) * SUB, : sizes.rows] + b3[g] for g in range(3)]
            here = slice(start, start + SUB)
            out_ref[0, s, here, :] = yz[0]
            out_ref[1, s, here, :] = 0.5 * (xy_ref[0, s, here, :] + yz[1])
            out_ref[2, s, here, :] = xy_ref[1, s, here, :]
            out_ref[3, s, here, :] = 0.5 * (xy_ref[2, s, here, :] + yz[2])


def call(kernel, name, outs, args, scratch=(), flops=0):
    single = not isinstance(outs, list)
    shapes = [jax.ShapeDtypeStruct(shape, kind) for shape, kind in ([outs] if single else outs)]
    return pl.pallas_call(
        kernel,
        name=name,
        out_shape=shapes[0] if single else shapes,
        scratch_shapes=scratch,
        compiler_params=pltpu.CompilerParams(vmem_limit_bytes=LIMIT),
        cost_estimate=pl.CostEstimate(flops=flops, bytes_accessed=1 << 20, transcendentals=0),
    )(*args)


def local(image, first_kernel, first_bias, middle_kernel, middle_bias, last_kernel, last_bias):
    slices, rows, cols = image.shape
    channels, outputs = first_kernel.shape[2], last_kernel.shape[2]
    sizes = Sizes(slices, rows, cols, channels, outputs, lax.axis_size("slab"), lax.axis_size("row"))
    t = image.transpose(0, 2, 1)
    even, odd = swap_rows(t, 0), swap_rows(t, 1)
    own, *weights = call(
        functools.partial(prepare_kernel, sizes),
        "prepare",
        [(t.shape, BF16), *sizes.weight_shapes()],
        (
            t,
            first_kernel.reshape(3, 3, channels),
            first_bias.reshape(1, channels),
            middle_kernel,
            middle_bias.reshape(1, channels),
            last_kernel,
            last_bias.reshape(1, outputs),
        ),
        flops=1 << 20,
    )
    wide = rows + 6
    e = call(extend_kernel, "extend", ((slices, cols, wide), BF16), (own, even, odd))
    even, odd = swap_slabs(e, 0), swap_slabs(e, 1)
    lanes = max(kind[2][1] for kind in sizes.kinds) * channels
    xy_hidden = pltpu.VMEM(((sizes.span + 2) * SUB, LANES), F32)
    yz_hidden = pltpu.VMEM(((rows + 2) * SUB, LANES), F32)
    xy = call(
        functools.partial(xy_kernel, sizes),
        "xy",
        ((outputs, slices, cols, rows), F32),
        (e, *weights[5:]),
        [xy_hidden] * pl.cdiv(lanes, LANES),
        flops=1 << 28,
    )
    flows = call(
        functools.partial(yz_kernel, sizes),
        "yz",
        ((outputs + 1, slices, cols, rows), F32),
        (e, even, odd, xy, *weights[:5], weights[-1]),
        [pltpu.VMEM((outputs * slices * SUB, LANES), F32)]
        + [yz_hidden] * pl.cdiv((slices + 2) * channels, LANES),
        flops=1 << 28,
    )
    return flows.transpose(0, 1, 3, 2)


def solution(mesh):
    placed = (P("slab", "row", None), P(), P(), P(), P(), P(), P())
    return jax.shard_map(
        local, mesh=mesh, in_specs=placed, out_specs=P(None, "slab", "row", None), check_vma=False
    )
```

time: 53 us -> 14.5 us (0.27)
  the two profiles are of different devices: /device:TPU:1 before, /device:TPU:0 now
where the time goes in v1:
time: 14.5 us; the launch traced here: 14.3 us
  starting transfers between devices  6.17 us (43%)
  local copies, waits for them, and re-layouts  4.23 us (29%)
  Pallas kernels  3.1 us (21%)
  waiting for transfers between devices  0.72 us (5%)
    unnamed x14, local copies, waits for them, and re-layouts  4.23 us
    ppermute x2, starting transfers between devices, swap_rows(): return lax.ppermute(values, 'row', sorted(partner.items()))  3.11 us
    pallas_call x4, Pallas kernels, call(): pl.pallas_call(kernel, name=name, out_shape=shapes[0] if single else shap...  3.1 us
    ppermute x2, starting transfers between devices, swap_slabs(): return lax.ppermute(values, ('slab', 'row'), pairs)  3.06 us
    ppermute x2, waiting for transfers between devices, swap_slabs(): return lax.ppermute(values, ('slab', 'row'), pairs)  0.71 us
  transfers between devices with their start and end apart: 4, of which 1 were waited for; matrix products, arithmetic and copies ran while one was open for 0% of the time, Pallas kernels for 9%

profile of v1, /device:TPU:0, one launch (start us, length us, event | category | flops | bytes accessed | tf_op | source)
XLA Modules:
  0.0 14.3 jit_solution(15861210464659309280)
XLA Ops:
  0.0 0.0 copy-start.1
  0.0 2.4 %collective-permute-start.1 = (bf16[4,8,32]{2,1,0:T(8,128)(2,1)}, bf16[4,8,32]{2,1,0:T(8,128)(2,1)S(1)}, u32[]{:S(2)}, u32[]{:S(2)}) collective-permute-start(bf16[4,8,32]{2,1,0:T(8,128)(2,1)} %bitcast.6), channel_id=1, source_target_pairs={{0,3},{1,2},{2,1},{3,0},{4,7},{5,6},{6,5},{7,4},{8,11},{9,10},{10,... | collective-permute-start | bytes 6152 | tf_op jit(solution)/shard_map/ppermute | solution.py:32
  2.4 0.7 %collective-permute-start = (bf16[4,8,32]{2,1,0:T(8,128)(2,1)}, bf16[4,8,32]{2,1,0:T(8,128)(2,1)S(1)}, u32[]{:S(2)}, u32[]{:S(2)}) collective-permute-start(bf16[4,8,32]{2,1,0:T(8,128)(2,1)} %bitcast.7), channel_id=1, source_target_pairs={{0,1},{1,0},{2,3},{3,2},{4,5},{5,4},{6,7},{7,6},{8,9},{9,8},{10,11... | collective-permute-start | bytes 6152 | tf_op jit(solution)/shard_map/ppermute | solution.py:32
  3.1 0.0 copy-done.1
  3.1 0.0 copy-start
  3.1 0.9 %copy-done = bf16[3,3,32,32]{3,2,1,0:T(8,128)(2,1)S(1)} copy-done((bf16[3,3,32,32]{3,2,1,0:T(8,128)(2,1)S(1)}, bf16[3,3,32,32]{3,2,1,0:T(8,128)(2,1)}, u32[]{:S(2)}) %copy-start) | copy-done | bytes 18456
  4.0 0.0 copy-start.2
  4.0 0.7 %copy-done.2 = bf16[4,32,8]{1,2,0:T(8,128)(2,1)S(1)} copy-done((bf16[4,32,8]{1,2,0:T(8,128)(2,1)S(1)}, bf16[4,32,8]{1,2,0:T(8,128)(2,1)}, u32[]{:S(2)}) %copy-start.2) | copy-done | bytes 2072
  4.7 0.0 copy-start.3
  4.7 0.7 %copy-done.3 = bf16[3,3,32,1]{2,1,3,0:T(4,128)(2,1)S(1)} copy-done((bf16[3,3,32,1]{2,1,3,0:T(4,128)(2,1)S(1)}, bf16[3,3,32,1]{2,1,3,0:T(4,128)(2,1)}, u32[]{:S(2)}) %copy-start.3) | copy-done | bytes 600
  5.4 0.0 copy-start.4
  5.4 0.7 %copy-done.4 = f32[32]{0:T(128)S(1)} copy-done((f32[32]{0:T(128)S(1)}, f32[32]{0:T(128)}, u32[]{:S(2)}) %copy-start.4) | copy-done | bytes 152
  6.0 0.0 copy-start.5
  6.0 0.7 %copy-done.5 = f32[32]{0:T(128)S(1)} copy-done((f32[32]{0:T(128)S(1)}, f32[32]{0:T(128)}, u32[]{:S(2)}) %copy-start.5) | copy-done | bytes 152
  6.7 0.0 copy-start.6
  6.7 0.7 %copy-done.6 = f32[3]{0:T(128)S(1)} copy-done((f32[3]{0:T(128)S(1)}, f32[3]{0:T(128)}, u32[]{:S(2)}) %copy-start.6) | copy-done | bytes 36
  7.4 0.4 %prepare.1 = (bf16[4,8,32]{2,1,0:T(8,128)(2,1)S(1)}, bf16[3,96,256]{2,1,0:T(8,128)(2,1)S(1)}, bf16[3,192,256]{2,1,0:T(8,128)(2,1)S(1)}, bf16[3,12,192]{2,1,0:T(8...) custom-call(bf16[4,8,32]{2,1,0:T(8,128)(2,1)S(1)} %bitcast.8, ...), custom_call_target="tpu_custom_call" | custom-call | flops 1048576 | bytes 1048576 | tf_op jit(solution)/shard_map/prepare/pallas_call | solution.py:302
  7.7 0.0 collective-permute-done.1.odd_ref
  7.7 0.0 collective-permute-done.even_ref
  7.7 0.1 extend.1.e_ref
  7.8 0.0 collective-permute-start.3
  7.9 3.0 %collective-permute-start.2 = (bf16[4,8,38]{2,1,0:T(8,128)(2,1)S(1)}, bf16[4,8,38]{2,1,0:T(8,128)(2,1)S(1)}, u32[]{:S(2)}, u32[]{:S(2)}) collective-permute-start(bf16[4,8,38]{2,1,0:T(8,128)(2,1)S(1)} %extend.1.e_ref), channel_id=1, source_target_pairs={{0,4},{1,5},{2,6},{3,7},{4,0},{5,1},{6,2},{7,3},{8,12},{9,13},{10,... | collective-permute-start | bytes 7304 | tf_op jit(solution)/shard_map/ppermute | solution.py:44
  10.9 0.9 %xy.1.xy_ref = f32[3,4,8,32]{3,2,1,0:T(8,128)S(1)} custom-call(bf16[4,8,38]{2,1,0:T(8,128)(2,1)S(1)} %extend.1.e_ref, bf16[3,32,256]{2,1,0:T(8,128)(2,1)S(1)} %get-tuple-element.18.refs_0_, bf16[3,256,256]{2,1,0:T(8,128)(2,1)S(1)} %get-tuple-element.19.refs_1_, bf16[3,24,256]{2,1,0:T(8,128)(2,1)S(1)} %get-tuple-element.20.refs_2_, ...), custom_call_target="tpu_custom_call" | custom-call | flops 268435456 | bytes 1048576 | tf_op jit(solution)/shard_map/xy/pallas_call | solution.py:302
  11.8 0.0 collective-permute-done.3.odd_ref
  11.8 0.7 %collective-permute-done.2.even_ref = bf16[4,8,38]{2,1,0:T(8,128)(2,1)S(1)} collective-permute-done((bf16[4,8,38]{2,1,0:T(8,128)(2,1)S(1)}, bf16[4,8,38]{2,1,0:T(8,128)(2,1)S(1)}, u32[]{:S(2)}, u32[]{:S(2)}) %collective-permute-start.2) | collective-permute-done | bytes 2464 | tf_op jit(solution)/shard_map/ppermute | solution.py:44
  12.5 1.7 %yz.1 = f32[4,4,8,32]{3,2,1,0:T(8,128)} custom-call(bf16[4,8,38]{2,1,0:T(8,128)(2,1)S(1)} %extend.1.e_ref, bf16[4,8,38]{2,1,0:T(8,128)(2,1)S(1)} %collective-permute-done.2.even_ref, bf16[4,8,38]{2,1,0:T(8,128)(2,1)S(1)} %collective-permute-done.3.odd_ref, f32[3,4,8,32]{3,2,1,0:T(8,128)S(1)} %xy.1.xy_ref, bf16[3,96,256]{2,1,0:T(8,128)(2,1)S(1)} %get-tuple-element.24.w1, ...), custom_call_target="tpu_custom_call" | custom-call | flops 268435456 | bytes 1048576 | tf_op jit(solution)/shard_map/yz/pallas_call | solution.py:302
Async XLA Ops:
  0.0 3.1 %copy-start.1 = (bf16[3,3,3,32]{3,2,1,0:T(4,128)(2,1)S(1)}, bf16[3,3,3,32]{3,2,1,0:T(4,128)(2,1)}, u32[]{:S(2)}) copy-start(bf16[3,3,3,32]{3,2,1,0:T(4,128)(2,1)} %k3_ref.1) | copy-start | bytes 5188
  0.0 7.7 %collective-permute-start.1 = (bf16[4,8,32]{2,1,0:T(8,128)(2,1)}, bf16[4,8,32]{2,1,0:T(8,128)(2,1)S(1)}, u32[]{:S(2)}, u32[]{:S(2)}) collective-permute-start(bf16[4,8,32]{2,1,0:T(8,128)(2,1)} %bitcast.6), channel_id=1, source_target_pairs={{0,3},{1,2},{2,1},{3,0},{4,7},{5,6},{6,5},{7,4},{8,11},{9,10},{10,... | collective-permute-start | bytes 6152 | tf_op jit(solution)/shard_map/ppermute | solution.py:32
  2.4 5.3 %collective-permute-start = (bf16[4,8,32]{2,1,0:T(8,128)(2,1)}, bf16[4,8,32]{2,1,0:T(8,128)(2,1)S(1)}, u32[]{:S(2)}, u32[]{:S(2)}) collective-permute-start(bf16[4,8,32]{2,1,0:T(8,128)(2,1)} %bitcast.7), channel_id=1, source_target_pairs={{0,1},{1,0},{2,3},{3,2},{4,5},{5,4},{6,7},{7,6},{8,9},{9,8},{10,11... | collective-permute-start | bytes 6152 | tf_op jit(solution)/shard_map/ppermute | solution.py:32
  3.1 0.9 %copy-start = (bf16[3,3,32,32]{3,2,1,0:T(8,128)(2,1)S(1)}, bf16[3,3,32,32]{3,2,1,0:T(8,128)(2,1)}, u32[]{:S(2)}) copy-start(bf16[3,3,32,32]{3,2,1,0:T(8,128)(2,1)} %k2_ref.1) | copy-start | bytes 55300
  4.0 0.7 %copy-start.2 = (bf16[4,32,8]{1,2,0:T(8,128)(2,1)S(1)}, bf16[4,32,8]{1,2,0:T(8,128)(2,1)}, u32[]{:S(2)}) copy-start(bf16[4,32,8]{1,2,0:T(8,128)(2,1)} %param.7) | copy-start | bytes 6148
  4.7 0.7 %copy-start.3 = (bf16[3,3,32,1]{2,1,3,0:T(4,128)(2,1)S(1)}, bf16[3,3,32,1]{2,1,3,0:T(4,128)(2,1)}, u32[]{:S(2)}) copy-start(bf16[3,3,32,1]{2,1,3,0:T(4,128)(2,1)} %param.8) | copy-start | bytes 1732
  5.4 0.7 %copy-start.4 = (f32[32]{0:T(128)S(1)}, f32[32]{0:T(128)}, u32[]{:S(2)}) copy-start(f32[32]{0:T(128)} %param.9) | copy-start | bytes 388
  6.0 0.7 %copy-start.5 = (f32[32]{0:T(128)S(1)}, f32[32]{0:T(128)}, u32[]{:S(2)}) copy-start(f32[32]{0:T(128)} %param.11) | copy-start | bytes 388
  6.7 0.7 %copy-start.6 = (f32[3]{0:T(128)S(1)}, f32[3]{0:T(128)}, u32[]{:S(2)}) copy-start(f32[3]{0:T(128)} %param.13) | copy-start | bytes 40
  7.8 4.0 %collective-permute-start.3 = (bf16[4,8,38]{2,1,0:T(8,128)(2,1)S(1)}, bf16[4,8,38]{2,1,0:T(8,128)(2,1)S(1)}, u32[]{:S(2)}, u32[]{:S(2)}) collective-permute-start(bf16[4,8,38]{2,1,0:T(8,128)(2,1)S(1)} %extend.1.e_ref), channel_id=1, source_target_pairs={{0,1},{1,0},{2,3},{3,2},{4,8},{5,9},{6,10},{7,11},{8,4},{9,5},{10,... | collective-permute-start | bytes 7304 | tf_op jit(solution)/shard_map/ppermute | solution.py:44
  7.9 4.7 %collective-permute-start.2 = (bf16[4,8,38]{2,1,0:T(8,128)(2,1)S(1)}, bf16[4,8,38]{2,1,0:T(8,128)(2,1)S(1)}, u32[]{:S(2)}, u32[]{:S(2)}) collective-permute-start(bf16[4,8,38]{2,1,0:T(8,128)(2,1)S(1)} %extend.1.e_ref), channel_id=1, source_target_pairs={{0,4},{1,5},{2,6},{3,7},{4,0},{5,1},{6,2},{7,3},{8,12},{9,13},{10,... | collective-permute-start | bytes 7304 | tf_op jit(solution)/shard_map/ppermute | solution.py:44

commit v2 on v1

--- a/solution.py
+++ b/solution.py
@@ -147,9 +147,20 @@
     return total.astype(BF16)
 
 
-def prepare_kernel(sizes, t_ref, k1_ref, b1_ref, k2_ref, b2_ref, k3_ref, b3_ref, t_out, *outs):
+def prepare_kernel(sizes, *refs):
+    count = 7
+    arguments, outs, held, sems = refs[:count], refs[count:-count], refs[-count:-1], refs[-1]
+    t_out, *outs = outs
+    copies = [
+        pltpu.make_async_copy(here, there, sems.at[i])
+        for i, (here, there) in enumerate(zip(arguments, (t_out, *held)))
+    ]
+    for copy in copies:
+        copy.start()
+    for copy in copies:
+        copy.wait()
     c, z, n_out = sizes.channels, sizes.slices, sizes.outputs
-    t_out[...] = t_ref[...]
+    k1_ref, b1_ref, k2_ref, b2_ref, k3_ref, b3_ref = held
     k1 = k1_ref[...].astype(F32)
     k3 = k3_ref[...].astype(F32)
     b1, b2 = b1_ref[...], b2_ref[...]
@@ -296,13 +307,14 @@
             out_ref[3, s, here, :] = 0.5 * (xy_ref[2, s, here, :] + yz[2])
 
 
-def call(kernel, name, outs, args, scratch=(), flops=0):
+def call(kernel, name, outs, args, scratch=(), flops=0, space=pltpu.VMEM):
     single = not isinstance(outs, list)
     shapes = [jax.ShapeDtypeStruct(shape, kind) for shape, kind in ([outs] if single else outs)]
     return pl.pallas_call(
         kernel,
         name=name,
         out_shape=shapes[0] if single else shapes,
+        in_specs=[pl.BlockSpec(memory_space=space)] * len(args),
         scratch_shapes=scratch,
         compiler_params=pltpu.CompilerParams(vmem_limit_bytes=LIMIT),
         cost_estimate=pl.CostEstimate(flops=flops, bytes_accessed=1 << 20, transcendentals=0),
@@ -315,20 +327,22 @@
     sizes = Sizes(slices, rows, cols, channels, outputs, lax.axis_size("slab"), lax.axis_size("row"))
     t = image.transpose(0, 2, 1)
     even, odd = swap_rows(t, 0), swap_rows(t, 1)
+    parameters = (
+        first_kernel.reshape(3, 3, channels),
+        first_bias.reshape(1, channels),
+        middle_kernel,
+        middle_bias.reshape(1, channels),
+        last_kernel,
+        last_bias.reshape(1, outputs),
+    )
     own, *weights = call(
         functools.partial(prepare_kernel, sizes),
         "prepare",
         [(t.shape, BF16), *sizes.weight_shapes()],
-        (
-            t,
-            first_kernel.reshape(3, 3, channels),
-            first_bias.reshape(1, channels),
-            middle_kernel,
-            middle_bias.reshape(1, channels),
-            last_kernel,
-            last_bias.reshape(1, outputs),
-        ),
+        [pltpu.with_memory_space_constraint(p, pltpu.HBM) for p in (t, *parameters)],
+        [pltpu.VMEM(p.shape, p.dtype) for p in parameters] + [pltpu.SemaphoreType.DMA((7,))],
         flops=1 << 20,
+        space=pltpu.HBM,
     )
     wide = rows + 6
     e = call(extend_kernel, "extend", ((slices, cols, wide), BF16), (own, even, odd))

time: 14.5 us -> 11.5 us (0.79)
  local copies, waits for them, and re-layouts: 4.23 us -> 0 us
  Pallas kernels: 3.1 us -> 4.1 us
  starting transfers between devices: 6.17 us -> 6.44 us
    unnamed x14 -> x0, local copies, waits for them, and re-layouts: 4.23 us -> none
    pallas_call x4, Pallas kernels: 3.1 us -> 4.1 us  [call(): pl.pallas_call(kernel, name=name, out_shape=shapes[0] if single else shap...]
    ppermute x2, starting transfers between devices: 3.06 us -> 3.33 us  [swap_slabs(): return lax.ppermute(values, ('slab', 'row'), pairs)]
  transfers between devices with their start and end apart: 4 -> 4, of which waited for: 1 -> 1; matrix products, arithmetic and copies ran while one was open for 0% -> 0% of each run, Pallas kernels for 9% -> 20%
where the time goes in v2:
time: 11.5 us; the launch traced here: 11.3 us
  starting transfers between devices  6.44 us (56%)
  Pallas kernels  4.1 us (36%)
  waiting for transfers between devices  0.72 us (6%)
    pallas_call x4, Pallas kernels, call(): pl.pallas_call(kernel, name=name, out_shape=shapes[0] if single else shap...  4.1 us
    ppermute x2, starting transfers between devices, swap_slabs(): return lax.ppermute(values, ('slab', 'row'), pairs)  3.33 us
    ppermute x2, starting transfers between devices, swap_rows(): return lax.ppermute(values, 'row', sorted(partner.items()))  3.11 us
    ppermute x2, waiting for transfers between devices, swap_slabs(): return lax.ppermute(values, ('slab', 'row'), pairs)  0.72 us
  transfers between devices with their start and end apart: 4, of which 1 were waited for; matrix products, arithmetic and copies ran while one was open for 0% of the time, Pallas kernels for 20%

profile of v2, /device:TPU:0, one launch (start us, length us, event | category | flops | bytes accessed | tf_op | source)
XLA Modules:
  0.0 11.3 jit_solution(15676046393851280418)
XLA Ops:
  0.0 2.4 %collective-permute-start.1 = (bf16[4,8,32]{2,1,0:T(8,128)(2,1)}, bf16[4,8,32]{2,1,0:T(8,128)(2,1)S(1)}, u32[]{:S(2)}, u32[]{:S(2)}) collective-permute-start(bf16[4,8,32]{2,1,0:T(8,128)(2,1)} %bitcast.6), channel_id=1, source_target_pairs={{0,3},{1,2},{2,1},{3,0},{4,7},{5,6},{6,5},{7,4},{8,11},{9,10},{10,... | collective-permute-start | bytes 6152 | tf_op jit(solution)/shard_map/ppermute | solution.py:32
  2.4 0.7 %collective-permute-start = (bf16[4,8,32]{2,1,0:T(8,128)(2,1)}, bf16[4,8,32]{2,1,0:T(8,128)(2,1)S(1)}, u32[]{:S(2)}, u32[]{:S(2)}) collective-permute-start(bf16[4,8,32]{2,1,0:T(8,128)(2,1)} %bitcast.7), channel_id=1, source_target_pairs={{0,1},{1,0},{2,3},{3,2},{4,5},{5,4},{6,7},{7,6},{8,9},{9,8},{10,11... | collective-permute-start | bytes 6152 | tf_op jit(solution)/shard_map/ppermute | solution.py:32
  3.1 1.4 %prepare.1 = (bf16[4,8,32]{2,1,0:T(8,128)(2,1)S(1)}, bf16[3,96,256]{2,1,0:T(8,128)(2,1)S(1)}, bf16[3,192,256]{2,1,0:T(8,128)(2,1)S(1)}, bf16[3,12,192]{2,1,0:T(8...) custom-call(bf16[4,8,32]{2,1,0:T(8,128)(2,1)} %bitcast.8, ...), custom_call_target="tpu_custom_call" | custom-call | flops 1048576 | bytes 1048576 | tf_op jit(solution)/shard_map/prepare/pallas_call | solution.py:313
  4.5 0.0 collective-permute-done.1.odd_ref
  4.5 0.0 collective-permute-done.even_ref
  4.5 0.1 extend.1.e_ref
  4.6 0.2 %collective-permute-start.3 = (bf16[4,8,38]{2,1,0:T(8,128)(2,1)S(1)}, bf16[4,8,38]{2,1,0:T(8,128)(2,1)S(1)}, u32[]{:S(2)}, u32[]{:S(2)}) collective-permute-start(bf16[4,8,38]{2,1,0:T(8,128)(2,1)S(1)} %extend.1.e_ref), channel_id=1, source_target_pairs={{0,1},{1,0},{2,3},{3,2},{4,8},{5,9},{6,10},{7,11},{8,4},{9,5},{10,... | collective-permute-start | bytes 7304 | tf_op jit(solution)/shard_map/ppermute | solution.py:44
  4.7 3.2 %collective-permute-start.2 = (bf16[4,8,38]{2,1,0:T(8,128)(2,1)S(1)}, bf16[4,8,38]{2,1,0:T(8,128)(2,1)S(1)}, u32[]{:S(2)}, u32[]{:S(2)}) collective-permute-start(bf16[4,8,38]{2,1,0:T(8,128)(2,1)S(1)} %extend.1.e_ref), channel_id=1, source_target_pairs={{0,4},{1,5},{2,6},{3,7},{4,0},{5,1},{6,2},{7,3},{8,12},{9,13},{10,... | collective-permute-start | bytes 7304 | tf_op jit(solution)/shard_map/ppermute | solution.py:44
  7.9 0.9 %xy.1.xy_ref = f32[3,4,8,32]{3,2,1,0:T(8,128)S(1)} custom-call(bf16[4,8,38]{2,1,0:T(8,128)(2,1)S(1)} %extend.1.e_ref, bf16[3,32,256]{2,1,0:T(8,128)(2,1)S(1)} %get-tuple-element.18.refs_0_, bf16[3,256,256]{2,1,0:T(8,128)(2,1)S(1)} %get-tuple-element.19.refs_1_, bf16[3,24,256]{2,1,0:T(8,128)(2,1)S(1)} %get-tuple-element.20.refs_2_, ...), custom_call_target="tpu_custom_call" | custom-call | flops 268435456 | bytes 1048576 | tf_op jit(solution)/shard_map/xy/pallas_call | solution.py:313
  8.8 0.0 collective-permute-done.3.odd_ref
  8.8 0.7 %collective-permute-done.2.even_ref = bf16[4,8,38]{2,1,0:T(8,128)(2,1)S(1)} collective-permute-done((bf16[4,8,38]{2,1,0:T(8,128)(2,1)S(1)}, bf16[4,8,38]{2,1,0:T(8,128)(2,1)S(1)}, u32[]{:S(2)}, u32[]{:S(2)}) %collective-permute-start.2) | collective-permute-done | bytes 2464 | tf_op jit(solution)/shard_map/ppermute | solution.py:44
  9.5 1.7 %yz.1 = f32[4,4,8,32]{3,2,1,0:T(8,128)} custom-call(bf16[4,8,38]{2,1,0:T(8,128)(2,1)S(1)} %extend.1.e_ref, bf16[4,8,38]{2,1,0:T(8,128)(2,1)S(1)} %collective-permute-done.2.even_ref, bf16[4,8,38]{2,1,0:T(8,128)(2,1)S(1)} %collective-permute-done.3.odd_ref, f32[3,4,8,32]{3,2,1,0:T(8,128)S(1)} %xy.1.xy_ref, bf16[3,96,256]{2,1,0:T(8,128)(2,1)S(1)} %get-tuple-element.24.w1, ...), custom_call_target="tpu_custom_call" | custom-call | flops 268435456 | bytes 1048576 | tf_op jit(solution)/shard_map/yz/pallas_call | solution.py:313
Async XLA Ops:
  0.0 4.5 %collective-permute-start.1 = (bf16[4,8,32]{2,1,0:T(8,128)(2,1)}, bf16[4,8,32]{2,1,0:T(8,128)(2,1)S(1)}, u32[]{:S(2)}, u32[]{:S(2)}) collective-permute-start(bf16[4,8,32]{2,1,0:T(8,128)(2,1)} %bitcast.6), channel_id=1, source_target_pairs={{0,3},{1,2},{2,1},{3,0},{4,7},{5,6},{6,5},{7,4},{8,11},{9,10},{10,... | collective-permute-start | bytes 6152 | tf_op jit(solution)/shard_map/ppermute | solution.py:32
  2.4 2.1 %collective-permute-start = (bf16[4,8,32]{2,1,0:T(8,128)(2,1)}, bf16[4,8,32]{2,1,0:T(8,128)(2,1)S(1)}, u32[]{:S(2)}, u32[]{:S(2)}) collective-permute-start(bf16[4,8,32]{2,1,0:T(8,128)(2,1)} %bitcast.7), channel_id=1, source_target_pairs={{0,1},{1,0},{2,3},{3,2},{4,5},{5,4},{6,7},{7,6},{8,9},{9,8},{10,11... | collective-permute-start | bytes 6152 | tf_op jit(solution)/shard_map/ppermute | solution.py:32
  4.6 4.2 %collective-permute-start.3 = (bf16[4,8,38]{2,1,0:T(8,128)(2,1)S(1)}, bf16[4,8,38]{2,1,0:T(8,128)(2,1)S(1)}, u32[]{:S(2)}, u32[]{:S(2)}) collective-permute-start(bf16[4,8,38]{2,1,0:T(8,128)(2,1)S(1)} %extend.1.e_ref), channel_id=1, source_target_pairs={{0,1},{1,0},{2,3},{3,2},{4,8},{5,9},{6,10},{7,11},{8,4},{9,5},{10,... | collective-permute-start | bytes 7304 | tf_op jit(solution)/shard_map/ppermute | solution.py:44
  4.7 4.8 %collective-permute-start.2 = (bf16[4,8,38]{2,1,0:T(8,128)(2,1)S(1)}, bf16[4,8,38]{2,1,0:T(8,128)(2,1)S(1)}, u32[]{:S(2)}, u32[]{:S(2)}) collective-permute-start(bf16[4,8,38]{2,1,0:T(8,128)(2,1)S(1)} %extend.1.e_ref), channel_id=1, source_target_pairs={{0,4},{1,5},{2,6},{3,7},{4,0},{5,1},{6,2},{7,3},{8,12},{9,13},{10,... | collective-permute-start | bytes 7304 | tf_op jit(solution)/shard_map/ppermute | solution.py:44
